TPU v7x, 256 devices: a whole 4x4x8 slice. The times are simulated.
256 devices in a mesh: row: 32 (over x, y, z_lo), src: 8 (over z_hi, core).
Axes of the slice: x: 4, y: 4, z: 8 (z_hi: 4, z_lo: 2; z = z_hi * 2 + z_lo), core: 2. Of those that a mesh axis runs over, the one named last changes fastest.
Arguments:
- traces: bfloat16 [16384, 128, 512], P('row', 'src'), may hold values from -6 to 6
- row_source: int32 [16384], P('row'), may hold values from 0 to 16383, as said below
- slice_data: bfloat16 [2, 16384, 32, 512], P(None, 'row', None, 'src'), may hold values from -0.03125 to 0.03125
- wavelet_inverse: float32 [2], replicated, may hold values from 0.3 to 0.8
Outputs:
- multiples: float32 [16384, 2, 128], P(('row', 'src'))
- primaries: float32 [16384, 2, 128], P(('row', 'src'))
Inputs may be any that keep to these rules, and one draw needn't show every extreme that they name: `row_source`: every recording row is named exactly once; entry e * 512 + p names a recording row whose index modulo 512 lies in [e * 16, (e + 1) * 16).
All inputs are finite; a program needn't handle non-finite values.
Results may differ from a plain program's by a relative error of at most 0.0056.
Values may be sent and summed in bfloat16 or wider, within the bound.
A program may use at most 64 MiB of HBM per device.

v0:
```python
import jax
import jax.numpy as jnp
from jax import lax
from jax.sharding import PartitionSpec as P

FREQ = 61
ITERS = 3


def dft_kernel(samples):
    ticks = jnp.arange(samples, dtype=jnp.int32)
    moment = ticks.astype(jnp.float32)
    ramp_len = samples // 8
    rising = 0.5 - 0.5 * jnp.cos(jnp.pi * (moment + 0.5) / ramp_len)
    falling = 0.5 - 0.5 * jnp.cos(jnp.pi * (samples - moment - 0.5) / ramp_len)
    taper = jnp.where(
        ticks < ramp_len,
        rising,
        jnp.where(ticks >= samples - ramp_len, falling, jnp.ones_like(rising)),
    )
    wrapped = ticks * FREQ % samples
    angles = 2.0 * jnp.pi / samples * wrapped.astype(jnp.float32)
    factor = 1.0 / jnp.sqrt(jnp.float32(samples))
    table = jnp.stack([taper * jnp.cos(angles) * factor, -taper * jnp.sin(angles) * factor], axis=1)
    return table.astype(jnp.bfloat16)


def combine_parts(real_terms, imag_terms, shot_count):
    pred_real = real_terms[:, :shot_count] - imag_terms[:, shot_count:]
    pred_imag = real_terms[:, shot_count:] + imag_terms[:, :shot_count]
    return jnp.stack([pred_real, pred_imag], axis=1)


def body(traces, row_source, slice_data, wavelet_inverse):
    block_rows, shot_local, samples = traces.shape
    kernel = dft_kernel(samples)
    spectra = jnp.dot(
        traces.reshape(block_rows * shot_local, samples), kernel, preferred_element_type=jnp.float32
    )
    spectra = jnp.transpose(spectra.reshape(block_rows, shot_local, 2), (0, 2, 1)).astype(
        jnp.bfloat16
    )
    arrived = lax.all_to_all(spectra, "row", split_axis=0, concat_axis=0, tiled=True)
    group_rows = block_rows // lax.axis_size("row")
    located = row_source // block_rows * group_rows + row_source % group_rows
    ordered = arrived[located]
    slice_rows = block_rows // lax.axis_size("src")
    panel = lax.all_to_all(ordered, "src", split_axis=0, concat_axis=2, tiled=True)
    shot_count = panel.shape[2]
    base = panel.astype(jnp.float32)
    wave_real = wavelet_inverse[0]
    wave_imag = wavelet_inverse[1]
    real_data = slice_data[0].reshape(block_rows, -1)
    imag_data = slice_data[1].reshape(block_rows, -1)
    estimate = panel
    predicted = jnp.zeros((slice_rows, 2, shot_count), jnp.float32)
    primaries = base
    for iteration in range(ITERS):
        shard_rows = lax.all_gather(estimate, "row", axis=0, tiled=True)
        piece_rows = shard_rows.shape[0]
        stacked = shard_rows.reshape(piece_rows, 2 * shot_count)
        real_terms = jnp.dot(real_data, stacked, preferred_element_type=jnp.float32)
        imag_terms = jnp.dot(imag_data, stacked, preferred_element_type=jnp.float32)
        summed = lax.psum(combine_parts(real_terms, imag_terms, shot_count), "src")
        predicted = lax.dynamic_slice_in_dim(
            summed, lax.axis_index("src") * slice_rows, slice_rows, 0
        )
        next_real = base[:, 0] - (wave_real * predicted[:, 0] - wave_imag * predicted[:, 1])
        next_imag = base[:, 1] - (wave_real * predicted[:, 1] + wave_imag * predicted[:, 0])
        primaries = jnp.stack([next_real, next_imag], axis=1)
        estimate = primaries.astype(jnp.bfloat16)
    return (predicted, primaries)


def solution(mesh):
    in_specs = (P("row", "src", None), P("row"), P(None, "row", None, "src"), P())
    out_specs = (P(("row", "src"), None, None), P(("row", "src"), None, None))
    return jax.shard_map(body, mesh=mesh, in_specs=in_specs, out_specs=out_specs, check_vma=False)
```

profile of v0, /device:TPU:2, one launch (start us, length us, event | category | flops | bytes accessed | tf_op | source)
XLA Modules:
  0.0 753.8 jit_solution(3112653908474504425)
XLA Ops:
  7.2 0.1 multiply_convert_fusion
  7.3 0.0 copy-start
  7.3 5.6 fusion
  12.9 0.2 convert_element_type.54
  13.2 0.3 copy.48
  13.5 0.9 reshape.153
  14.3 9.0 %all-to-all-start = ((bf16[32,2,256]{2,1,0:T(2,128)(2,1)}), bf16[32,2,256]{2,1,0:T(2,128)(2,1)S(1)}, u32[]{:S(2)}, u32[]{:S(2)}) async-start(bf16[32,2,256]{2,1,0:T(2,128)(2,1)} %reshape.153), calls=%async_computation | async-start | bytes 65536 | tf_op jit(solution)/shard_map/all_to_all | solution.py:43
  23.3 0.0 all-gather.4.cloned.1.call-start
  23.4 0.0 copy-done
  23.4 7.0 all-to-all-done
  30.4 0.2 reshape.154
  30.6 2.1 gather_fusion
  32.7 0.3 reshape.155
  33.0 15.2 %all_to_all.23 = bf16[8,2,1024]{2,1,0:T(2,128)(2,1)S(1)} all-to-all(bf16[8,2,1024]{2,1,0:T(2,128)(2,1)S(1)} %reshape.155), channel_id=1, replica_groups=mesh['row'=32,'src'=8] {'src'}, dimensions={0} | all-to-all | bytes 65536 | tf_op jit(solution)/shard_map/all_to_all | solution.py:48
  48.3 0.2 reshape.156
  48.5 0.2 copy.14
  48.6 0.7 copy.15
  49.4 0.0 all-gather.4.cloned.1.call-update
  49.4 0.0 all-reduce.4.cloned.1.call-start
  49.4 4.0 fusion.41
  53.4 136.0 %all-gather.4.cloned.1.call-done = bf16[2048,2,128]{2,1,0:T(2,128)(2,1)} async-done(((bf16[64,2,128]{2,1,0:T(2,128)(2,1)}), bf16[2048,2,128]{2,1,0:T(2,128)(2,1)}) %all-gather.4.cloned.1.call-update) | async-done | bytes 1048592 | tf_op jit(solution)/shard_map/all_gather | solution.py:59
  189.4 0.0 copy-start.2
  189.4 2.7 convolution_bitcast_fusion.4
  192.1 0.0 copy-done.2
  192.1 0.7 convolution_bitcast_fusion.5
  192.9 0.0 copy-start.1
  192.9 0.1 fusion.18
  193.0 0.8 pad_maximum_fusion
  193.8 0.0 all-reduce.4.cloned.1.call-update
  193.9 0.0 all-gather.6.cloned.1.call-start
  193.9 0.0 copy-done.1
  193.9 0.6 fusion.42
  194.5 80.9 %all-reduce.4.cloned.1.call-done = f32[512,2,128]{0,2,1:T(8,128)} async-done(((f32[512,2,128]{0,2,1:T(8,128)}), f32[512,2,128]{0,2,1:T(8,128)}) %all-reduce.4.cloned.1.call-update) | async-done | bytes 524304 | tf_op jit(solution)/shard_map/psum | solution.py:64
  275.5 2.1 subtract_convert_fusion.3
  277.6 0.7 copy.16
  278.4 0.0 all-gather.6.cloned.1.call-update
  278.4 0.0 all-reduce.6.cloned.1.call-start
  278.4 144.4 %all-gather.6.cloned.1.call-done = bf16[2048,2,128]{2,1,0:T(2,128)(2,1)} async-done(((bf16[64,2,128]{2,1,0:T(2,128)(2,1)}), bf16[2048,2,128]{2,1,0:T(2,128)(2,1)}) %all-gather.6.cloned.1.call-update) | async-done | bytes 1048592 | tf_op jit(solution)/shard_map/all_gather | solution.py:59
  422.9 0.0 copy-start.4
  422.9 2.7 convolution_bitcast_fusion.2
  425.6 0.0 copy-done.4
  425.6 0.7 convolution_bitcast_fusion.3
  426.4 0.1 fusion.16
  426.5 0.8 pad_maximum_fusion.1
  427.3 0.0 all-reduce.6.cloned.1.call-update
  427.3 0.0 all-gather.8.cloned.1.call-start
  427.4 81.5 %all-reduce.6.cloned.1.call-done = f32[512,2,128]{0,2,1:T(8,128)} async-done(((f32[512,2,128]{0,2,1:T(8,128)}), f32[512,2,128]{0,2,1:T(8,128)}) %all-reduce.6.cloned.1.call-update) | async-done | bytes 524304 | tf_op jit(solution)/shard_map/psum | solution.py:64
  508.8 2.1 subtract_convert_fusion.1
  511.0 0.7 copy.17
  511.7 0.0 all-gather.8.cloned.1.call-update
  511.8 0.0 all-reduce.8.cloned.1.call-start
  511.8 144.4 %all-gather.8.cloned.1.call-done = bf16[2048,2,128]{2,1,0:T(2,128)(2,1)} async-done(((bf16[64,2,128]{2,1,0:T(2,128)(2,1)}), bf16[2048,2,128]{2,1,0:T(2,128)(2,1)}) %all-gather.8.cloned.1.call-update) | async-done | bytes 1048592 | tf_op jit(solution)/shard_map/all_gather | solution.py:59
  656.3 0.0 copy-start.3
  656.3 2.7 convolution_bitcast_fusion
  659.0 0.0 copy-done.3
  659.0 0.7 convolution_bitcast_fusion.1
  659.8 0.1 fusion.14
  659.8 0.8 pad_maximum_fusion.2
  660.7 0.0 all-reduce.8.cloned.1.call-update
  660.7 81.6 %all-reduce.8.cloned.1.call-done = f32[512,2,128]{0,2,1:T(8,128)} async-done(((f32[512,2,128]{0,2,1:T(8,128)}), f32[512,2,128]{0,2,1:T(8,128)}) %all-reduce.8.cloned.1.call-update) | async-done | bytes 524304 | tf_op jit(solution)/shard_map/psum | solution.py:64
  742.3 1.0 constant_dynamic-slice_fusion
  743.3 0.7 copy.18
  744.0 2.1 subtract_subtract_fusion
  746.2 0.7 copy.19
  (6 shorter events, 0.1 us)
Async XLA Ops:
  7.3 16.1 %copy-start = (s32[512]{0:T(512)S(1)}, s32[512]{0:T(512)}, u32[]{:S(2)}) copy-start(s32[512]{0:T(512)} %param.5) | copy-start | bytes 6148
  14.3 16.1 %all-to-all-start = ((bf16[32,2,256]{2,1,0:T(2,128)(2,1)}), bf16[32,2,256]{2,1,0:T(2,128)(2,1)S(1)}, u32[]{:S(2)}, u32[]{:S(2)}) async-start(bf16[32,2,256]{2,1,0:T(2,128)(2,1)} %reshape.153), calls=%async_computation | async-start | bytes 65536 | tf_op jit(solution)/shard_map/all_to_all | solution.py:43
  23.3 166.1 %all-gather.4.cloned.1.call-start = ((), (), s32[]{:S(2)}) async-start(), calls=%async_computation.2 | async-start | bytes 1081344 | tf_op jit(solution)/shard_map/all_gather | solution.py:59
  49.4 226.1 %all-reduce.4.cloned.1.call-start = ((), (), s32[]{:S(2)}) async-start(), calls=%async_computation.3 | async-start | bytes 1048576 | tf_op jit(solution)/shard_map/psum | solution.py:64
  189.4 2.7 copy-start.2
  192.9 1.0 copy-start.1
  193.9 229.0 %all-gather.6.cloned.1.call-start = ((), (), s32[]{:S(2)}) async-start(), calls=%async_computation.4 | async-start | bytes 1081344 | tf_op jit(solution)/shard_map/all_gather | solution.py:59
  278.4 230.5 %all-reduce.6.cloned.1.call-start = ((), (), s32[]{:S(2)}) async-start(), calls=%async_computation.5 | async-start | bytes 1048576 | tf_op jit(solution)/shard_map/psum | solution.py:64
  422.9 2.7 copy-start.4
  427.3 229.0 %all-gather.8.cloned.1.call-start = ((), (), s32[]{:S(2)}) async-start(), calls=%async_computation.6 | async-start | bytes 1081344 | tf_op jit(solution)/shard_map/all_gather | solution.py:59
  511.8 230.6 %all-reduce.8.cloned.1.call-start = ((), (), s32[]{:S(2)}) async-start(), calls=%async_computation.7 | async-start | bytes 1048576 | tf_op jit(solution)/shard_map/psum | solution.py:64
  656.3 2.7 copy-start.3
Sparse Core Ops, SparseCore 0:
  49.5 139.8 all-gather.3
  194.0 81.4 all-reduce.3
  278.5 144.3 all-gather.5
  427.4 81.3 all-reduce.5
  511.9 144.3 all-gather.7
  660.8 81.4 all-reduce.7
where the time goes:
time: 754 us
  waiting for transfers between devices  676 us (90%)
  matrix products  16 us (2%)
  blocking collectives  15.2 us (2%)
  between operations  14.4 us (2%)
  local copies, waits for them, and re-layouts  13.5 us (2%)
  other arithmetic  9.38 us (1%)
  starting transfers between devices  9.22 us (1%)
    all_gather x3, waiting for transfers between devices, body(): shard_rows = lax.all_gather(estimate, 'row', axis=0, tiled=True)  425 us
    psum x3, waiting for transfers between devices, body(): summed = lax.psum(combine_parts(real_terms, imag_terms, shot_count), 'src')  244 us
    all_to_all x1, blocking collectives, body(): lax.all_to_all(ordered, 'src', split_axis=0, concat_axis=2, tiled=True)  15.2 us
  transfers between devices with their start and end apart: 7, of which 7 were waited for; matrix products, arithmetic and copies ran while one was open for 1% of the time, Pallas kernels for 0%

commit v1 on v0

--- a/solution.py
+++ b/solution.py
@@ -56,7 +56,9 @@
     predicted = jnp.zeros((slice_rows, 2, shot_count), jnp.float32)
     primaries = base
     for iteration in range(ITERS):
-        shard_rows = lax.all_gather(estimate, "row", axis=0, tiled=True)
+        shard_rows = jnp.concatenate(
+            lax.all_to_all(jnp.stack([estimate] * lax.axis_size("row")), "row", 0, 0), axis=0
+        )
         piece_rows = shard_rows.shape[0]
         stacked = shard_rows.reshape(piece_rows, 2 * shot_count)
         real_terms = jnp.dot(real_data, stacked, preferred_element_type=jnp.float32)

time: 754 us -> 356 us (0.47)
  waiting for transfers between devices: 676 us -> 232 us
  blocking collectives: 15.2 us -> 58.6 us
    all_gather x3 -> x0, waiting for transfers between devices: 425 us -> none  [body(): shard_rows = lax.all_gather(estimate, 'row', axis=0, tiled=True)]
    all_to_all x0 -> x2, blocking collectives: none -> 43.3 us  [body(): lax.all_to_all(jnp.stack([estimate] * lax.axis_size('row')), 'row', 0, 0)]
    psum x3, waiting for transfers between devices: 244 us -> 213 us  [body(): summed = lax.psum(combine_parts(real_terms, imag_terms, shot_count), 'src')]
    all_to_all x0 -> x1, waiting for transfers between devices: none -> 11.5 us  [body(): lax.all_to_all(jnp.stack([estimate] * lax.axis_size('row')), 'row', 0, 0)]
  transfers between devices with their start and end apart: 7 -> 5, of which waited for: 7 -> 5; matrix products, arithmetic and copies ran while one was open for 1% -> 1% of each run, Pallas kernels for 0% -> 0%
where the time goes in v1:
time: 356 us
  waiting for transfers between devices  232 us (65%)
  blocking collectives  58.6 us (16%)
  local copies, waits for them, and re-layouts  15.6 us (4%)
  starting transfers between devices  14.1 us (4%)
  between operations  14 us (4%)
  matrix products  11.7 us (3%)
  other arithmetic  9.91 us (3%)
    psum x3, waiting for transfers between devices, body(): summed = lax.psum(combine_parts(real_terms, imag_terms, shot_count), 'src')  213 us
    all_to_all x2, blocking collectives, body(): lax.all_to_all(jnp.stack([estimate] * lax.axis_size('row')), 'row', 0, 0)  43.3 us
    all_to_all x1, blocking collectives, body(): lax.all_to_all(ordered, 'src', split_axis=0, concat_axis=2, tiled=True)  15.2 us
    all_to_all x1, waiting for transfers between devices, body(): lax.all_to_all(jnp.stack([estimate] * lax.axis_size('row')), 'row', 0, 0)  11.5 us
    all_to_all x1, starting transfers between devices, body(): lax.all_to_all(spectra, 'row', split_axis=0, concat_axis=0, tiled=True)  8.97 us
  transfers between devices with their start and end apart: 5, of which 5 were waited for; matrix products, arithmetic and copies ran while one was open for 1% of the time, Pallas kernels for 0%

profile of v1, /device:TPU:2, one launch (start us, length us, event | category | flops | bytes accessed | tf_op | source)
XLA Modules:
  0.0 355.7 jit_solution(6910822759453488916)
XLA Ops:
  7.2 0.1 multiply_convert_fusion
  7.3 0.0 copy-start.2
  7.3 5.6 %fusion = bf16[8192,2]{0,1:T(2,128)(2,1)S(1)} fusion(bf16[8192,512]{1,0:T(8,128)(2,1)} %bitcast.69, bf16[512,1]{0,1:T(2,128)(2,1)S(1)} %get-tuple-element.24, bf16[512,1]{0,1:T(2,128)(2,1)S(1)} %get-tuple-element.25), kind=kOutput, calls=%fused_computation.2 | convolution fusion | flops 16797696 | bytes 8423424 | tf_op jit(solution)/shard_map/dot_general | solution.py:37
  12.9 0.2 convert_element_type.58
  13.2 0.3 copy.54
  13.5 0.9 reshape.158
  14.3 9.0 %all-to-all-start = ((bf16[32,2,256]{2,1,0:T(2,128)(2,1)}), bf16[32,2,256]{2,1,0:T(2,128)(2,1)S(1)}, u32[]{:S(2)}, u32[]{:S(2)}) async-start(bf16[32,2,256]{2,1,0:T(2,128)(2,1)} %reshape.158), calls=%async_computation | async-start | bytes 65536 | tf_op jit(solution)/shard_map/all_to_all | solution.py:43
  23.3 0.0 copy-done.2
  23.3 7.1 %all-to-all-done = bf16[32,2,256]{2,1,0:T(2,128)(2,1)S(1)} async-done(((bf16[32,2,256]{2,1,0:T(2,128)(2,1)}), bf16[32,2,256]{2,1,0:T(2,128)(2,1)S(1)}, u32[]{:S(2)}, u32[]{:S(2)}) %all-to-all-start) | async-done | bytes 32800 | tf_op jit(solution)/shard_map/all_to_all | solution.py:43
  30.4 0.2 reshape.159
  30.6 2.1 gather_fusion
  32.7 0.3 reshape.160
  33.0 15.2 %all_to_all.38 = bf16[8,2,1024]{2,1,0:T(2,128)(2,1)S(1)} all-to-all(bf16[8,2,1024]{2,1,0:T(2,128)(2,1)S(1)} %reshape.160), channel_id=1, replica_groups=mesh['row'=32,'src'=8] {'src'}, dimensions={0} | all-to-all | bytes 65536 | tf_op jit(solution)/shard_map/all_to_all | solution.py:48
  48.3 0.2 reshape.161
  48.5 0.2 copy.20
  48.6 0.1 copy.21
  48.7 1.9 stack.34
  50.7 5.0 %all-to-all-start.2 = ((bf16[32,64,2,128]{3,2,1,0:T(2,128)(2,1)}), bf16[32,64,2,128]{3,2,1,0:T(2,128)(2,1)S(1)}, u32[]{:S(2)}, u32[]{:S(2)}) async-start(bf16[32,64,2,128]{3,2,1,0:T(2,128)(2,1)} %stack.34), calls=%async_computation.2 | async-start | bytes 2097152 | tf_op jit(solution)/shard_map/all_to_all | solution.py:60
  55.7 0.0 all-reduce.4.cloned.1.call-start
  55.7 4.1 %fusion.41 = (bf16[1,512,32,64]{1,3,2,0:T(8,128)(2,1)S(1)}, bf16[1,512,32,64]{1,3,2,0:T(8,128)(2,1)}) fusion(bf16[2,512,32,64]{1,3,2,0:T(8,128)(2,1)} %param.6), kind=kLoop, calls=%fused_computation.88 | loop fusion | bytes 8388608 | tf_op jit(solution)/shard_map/slice | solution.py:53
  59.8 11.5 %all-to-all-done.2 = bf16[32,64,2,128]{3,2,1,0:T(2,128)(2,1)S(1)} async-done(((bf16[32,64,2,128]{3,2,1,0:T(2,128)(2,1)}), bf16[32,64,2,128]{3,2,1,0:T(2,128)(2,1)S(1)}, u32[]{:S(2)}, u32[]{:S(2)}) %all-to-all-start.2) | async-done | bytes 1048608 | tf_op jit(solution)/shard_map/all_to_all | solution.py:60
  71.3 2.3 convolution_bitcast_fusion.4
  73.6 0.7 convolution_bitcast_fusion.5
  74.3 0.0 copy-start.3
  74.4 0.1 fusion.18
  74.4 0.8 pad_maximum_fusion
  75.3 0.0 all-reduce.4.cloned.1.call-update
  75.3 0.0 all-reduce.6.cloned.1.call-start
  75.4 0.0 copy-done.3
  75.4 0.7 fusion.42
  76.1 68.6 %all-reduce.4.cloned.1.call-done = f32[512,2,128]{0,2,1:T(8,128)} async-done(((f32[512,2,128]{0,2,1:T(8,128)}), f32[512,2,128]{0,2,1:T(8,128)}) %all-reduce.4.cloned.1.call-update) | async-done | bytes 524304 | tf_op jit(solution)/shard_map/psum | solution.py:66
  144.6 2.3 subtract_convert_fusion.3
  147.0 0.1 copy.22
  147.1 0.0 copy-start
  147.1 0.9 stack.39
  148.0 21.7 %all_to_all.39 = bf16[32,64,2,128]{3,2,1,0:T(2,128)(2,1)S(1)} all-to-all(bf16[32,64,2,128]{3,2,1,0:T(2,128)(2,1)S(1)} %stack.39), channel_id=1, replica_groups=mesh['row'=32,'src'=8] {'row'}, dimensions={0} | all-to-all | bytes 2097152 | tf_op jit(solution)/shard_map/all_to_all | solution.py:60
  169.7 0.0 copy-done
  169.7 0.7 convolution_bitcast_fusion.2
  170.4 0.7 convolution_bitcast_fusion.3
  171.2 0.1 fusion.16
  171.3 0.8 pad_maximum_fusion.1
  172.1 0.0 all-reduce.6.cloned.1.call-update
  172.1 0.0 all-reduce.8.cloned.1.call-start
  172.2 72.4 %all-reduce.6.cloned.1.call-done = f32[512,2,128]{0,2,1:T(8,128)} async-done(((f32[512,2,128]{0,2,1:T(8,128)}), f32[512,2,128]{0,2,1:T(8,128)}) %all-reduce.6.cloned.1.call-update) | async-done | bytes 524304 | tf_op jit(solution)/shard_map/psum | solution.py:66
  244.5 2.3 subtract_convert_fusion.1
  246.9 0.1 copy.23
  247.0 0.0 copy-start.1
  247.0 0.9 stack.44
  248.0 21.7 %all_to_all.40 = bf16[32,64,2,128]{3,2,1,0:T(2,128)(2,1)S(1)} all-to-all(bf16[32,64,2,128]{3,2,1,0:T(2,128)(2,1)S(1)} %stack.44), channel_id=1, replica_groups=mesh['row'=32,'src'=8] {'row'}, dimensions={0} | all-to-all | bytes 2097152 | tf_op jit(solution)/shard_map/all_to_all | solution.py:60
  269.6 0.0 copy-done.1
  269.6 0.7 convolution_bitcast_fusion
  270.4 0.7 convolution_bitcast_fusion.1
  271.1 0.1 fusion.14
  271.2 0.8 pad_maximum_fusion.2
  272.1 0.0 all-reduce.8.cloned.1.call-update
  272.1 72.3 %all-reduce.8.cloned.1.call-done = f32[512,2,128]{0,2,1:T(8,128)} async-done(((f32[512,2,128]{0,2,1:T(8,128)}), f32[512,2,128]{0,2,1:T(8,128)}) %all-reduce.8.cloned.1.call-update) | async-done | bytes 524304 | tf_op jit(solution)/shard_map/psum | solution.py:66
  344.4 1.0 constant_dynamic-slice_fusion
  345.4 0.7 copy.24
  346.1 2.3 subtract_subtract_fusion
  348.4 0.7 copy.25
  (6 shorter events, 0.1 us)
Async XLA Ops:
  7.3 16.0 %copy-start.2 = (s32[512]{0:T(512)S(1)}, s32[512]{0:T(512)}, u32[]{:S(2)}) copy-start(s32[512]{0:T(512)} %param.5) | copy-start | bytes 6148
  14.3 16.1 %all-to-all-start = ((bf16[32,2,256]{2,1,0:T(2,128)(2,1)}), bf16[32,2,256]{2,1,0:T(2,128)(2,1)S(1)}, u32[]{:S(2)}, u32[]{:S(2)}) async-start(bf16[32,2,256]{2,1,0:T(2,128)(2,1)} %reshape.158), calls=%async_computation | async-start | bytes 65536 | tf_op jit(solution)/shard_map/all_to_all | solution.py:43
  50.7 20.6 %all-to-all-start.2 = ((bf16[32,64,2,128]{3,2,1,0:T(2,128)(2,1)}), bf16[32,64,2,128]{3,2,1,0:T(2,128)(2,1)S(1)}, u32[]{:S(2)}, u32[]{:S(2)}) async-start(bf16[32,64,2,128]{3,2,1,0:T(2,128)(2,1)} %stack.34), calls=%async_computation.2 | async-start | bytes 2097152 | tf_op jit(solution)/shard_map/all_to_all | solution.py:60
  55.7 88.9 %all-reduce.4.cloned.1.call-start = ((), (), s32[]{:S(2)}) async-start(), calls=%async_computation.5 | async-start | bytes 1048576 | tf_op jit(solution)/shard_map/psum | solution.py:66
  74.3 1.0 copy-start.3
  75.3 169.2 %all-reduce.6.cloned.1.call-start = ((), (), s32[]{:S(2)}) async-start(), calls=%async_computation.6 | async-start | bytes 1048576 | tf_op jit(solution)/shard_map/psum | solution.py:66
  147.1 22.6 %copy-start = (bf16[1,512,32,64]{1,3,2,0:T(8,128)(2,1)S(1)}, bf16[1,512,32,64]{1,3,2,0:T(8,128)(2,1)}, u32[]{:S(2)}) copy-start(bf16[1,512,32,64]{1,3,2,0:T(8,128)(2,1)} %get-tuple-element.9) | copy-start | bytes 6291460
  172.1 172.2 %all-reduce.8.cloned.1.call-start = ((), (), s32[]{:S(2)}) async-start(), calls=%async_computation.7 | async-start | bytes 1048576 | tf_op jit(solution)/shard_map/psum | solution.py:66
  247.0 22.6 %copy-start.1 = (bf16[1,512,32,64]{1,3,2,0:T(8,128)(2,1)S(1)}, bf16[1,512,32,64]{1,3,2,0:T(8,128)(2,1)}, u32[]{:S(2)}) copy-start(bf16[1,512,32,64]{1,3,2,0:T(8,128)(2,1)} %get-tuple-element.9) | copy-start | bytes 6291460
Sparse Core Ops, SparseCore 0:
  75.4 69.1 all-reduce.3
  172.3 72.2 all-reduce.5
  272.2 72.1 all-reduce.7
